TPU v7x, 128 devices: a whole 4x4x4 slice. The times are simulated.
128 devices in a mesh: row: 4 (over y), col: 32 (over x, z, core).
Axes of the slice: x: 4, y: 4, z: 4, core: 2. Of those that a mesh axis runs over, the one named last changes fastest.
Arguments:
- vectors: float32 [16, 1048576], P(None, ('row', 'col')), may hold values from -6 to 6
- coords: float32 [3, 1048576], P(None, ('row', 'col')), may hold values from 0 to 1
- leaf_basis: bfloat16 [4096, 64, 256], P(('row', 'col')), may hold values from -0.375 to 0.375
- transfer: bfloat16 [8192, 4096], P(('row', 'col')), may hold values from -0.5 to 0.5
- coupling: bfloat16 [8192, 6, 4096], P(('row', 'col')), may hold values from -0.3125 to 0.3125
- near_list: int32 [4096, 8], P(('row', 'col')), may hold values from 0 to 4095, as said below
- near_count: int32 [4096], P(('row', 'col')), may hold values from 1 to 8, as said below
- local_list: int32 [8192, 6], P(('row', 'col')), may hold values from 1 to 8191, as said below
- top_transfer: bfloat16 [256, 4096], replicated, may hold values from -0.5 to 0.5
- top_coupling: bfloat16 [256, 2, 4096], replicated, may hold values from -0.5 to 0.5
- top_list: int32 [256, 2], replicated, may hold values from 1 to 255, as said below
Outputs:
- product: float32 [16, 1048576], P(None, ('row', 'col'))
Inputs may be any that keep to these rules, and one draw needn't show every extreme that they name: `near_list`: entry 0 of a leaf's list is the leaf itself; every entry names a leaf of the same device or of the device just before or after it in the order of row then col; entries past near_count are ignored. `near_count`: devices differ in how full their leaves' lists are. `local_list`: a slot's partners are slots of the same level of the subtrees of the same device or of the device just before or after it; the rows of slots 0 and 1 are ignored. `top_list`: a slot's partners are upper slots of the same level; rows 0 and 1 are ignored.
All inputs are finite; a program needn't handle non-finite values.
Results may differ from a plain program's by a relative error of at most 0.0003.
Values sent between devices are 32-bit elements; how exact they have to be, the bound alone decides.
No kernel may reach another device: no remote copies, remote signals or barrier semaphores. Data moves between devices by JAX's collectives and lax.ppermute only.
A program may use at most 128 MiB of HBM per device.

v0:
```python
import functools
import math

import jax
import jax.numpy as jnp
from jax import lax
from jax.experimental import pallas as pl
from jax.experimental.pallas import tpu as pltpu
from jax.sharding import PartitionSpec as P

AXES = ("row", "col")
BF = jnp.bfloat16
F32 = jnp.float32
LOG2E = 1.4426950408889634
LN2 = 0.6931471805599453
JITTER_SQ = 0.0001
SIGMA = math.sqrt(3.0) / 0.2 * LOG2E
LEAF, RANK, VECS, LEAF_DEV, NEAR, FAR = 256, 64, 16, 32, 8, 6
DEVICES = 128
ROWS = 32
PITCH = 9
PAIRS = 384
GROUP = 12
NN = (((1,), (0,)), ((), ()))
NT = (((1,), (1,)), ((), ()))
SMEM = pl.BlockSpec(memory_space=pltpu.SMEM)
VMEM = pl.BlockSpec(memory_space=pltpu.VMEM)
HBM = pl.BlockSpec(memory_space=pltpu.HBM)


def dot(a, b, dims=NN):
    return lax.dot_general(a, b, dims, preferred_element_type=F32)


def pieces(x):
    hi = x.astype(BF)
    lo = (x - hi.astype(F32)).astype(BF)
    return jnp.concatenate([hi, lo], axis=0)


def folded(y):
    half = y.shape[0] // 2
    return y[:half] + y[half:]


def low_lanes(shape):
    return lax.broadcasted_iota(jnp.int32, shape, 1) < RANK


def joined(a, b):
    return jnp.where(low_lanes(a.shape), a, b)


def swapped(x):
    return pltpu.roll(x, RANK, 1)


def order_matrix(transposed):
    row = lax.broadcasted_iota(jnp.int32, (128, 128), 1 if transposed else 0)
    col = lax.broadcasted_iota(jnp.int32, (128, 128), 0 if transposed else 1)
    at = col % RANK
    source = jnp.where(at < 32, 2 * at, 2 * at - 63) + (col // RANK) * RANK
    return jnp.where(row == source, 1.0, 0.0).astype(BF)


def unpack_rows(load, tiles, block):
    for i in range(ROWS):
        x = load(i).astype(F32)
        tiles[0, pl.ds(i * PITCH, 8), :] = x[:8]
        tiles[1, pl.ds(i * PITCH, 8), :] = x[8:]
    for s in range(16):
        block(s, tiles[s // 8, pl.ds(s % 8, ROWS, stride=PITCH), :])


def pack_transfer(load, tiles, order, write):
    held = [None] * 16

    def keep(s, x):
        held[s] = x.astype(BF)

    unpack_rows(load, tiles, keep)
    ordered = dot(jnp.concatenate(held, axis=0), order)
    for s in range(16):
        x = ordered[s * ROWS : (s + 1) * ROWS]
        y = swapped(x)
        parent_odd = (s // 2) % 2
        rows = [y, x] if parent_odd else [x, y]
        write(s // 2, s % 2, jnp.concatenate(rows, axis=0).astype(BF))


def pack_kernel(first, transfer, ee, tiles):
    order = order_matrix(False)

    def group(g, _):
        base = pl.multiple_of(first + g * 16, 16)

        def write(m, child, value):
            ee[g * 8 + m, pl.ds(child * RANK, RANK), :] = value

        pack_transfer(
            lambda i: transfer[pl.ds(base, 16), pl.ds(i * 128, 128)], tiles, order, write
        )
        return 0

    lax.fori_loop(0, transfer.shape[0] // 32, group, 0)


def blocks_kernel(coupling, blocks, tiles):
    for k in range(FAR):

        def group(g, _):
            base = pl.multiple_of(g * 16, 16)

            def write(s, c):
                y = swapped(c)
                rows = [y, c] if s % 2 else [c, y]
                blocks[g * 16 + s, k * RANK : (k + 1) * RANK, :] = jnp.concatenate(
                    rows, axis=0
                ).astype(BF)

            unpack_rows(
                lambda i: coupling[k, pl.ds(base, 16), pl.ds(i * 128, 128)], tiles, write
            )
            return 0

        lax.fori_loop(0, 2 * LEAF_DEV // 16, group, 0)


def pair_list(lists, counts, first):
    shape = lists.shape
    partner = lists - first
    live = lax.broadcasted_iota(jnp.int32, shape, 0) < counts
    local = live & (partner >= LEAF_DEV) & (partner < 2 * LEAF_DEV)
    before = lax.broadcasted_iota(jnp.int32, (LEAF_DEV, LEAF_DEV), 0)
    before = before < lax.broadcasted_iota(jnp.int32, (LEAF_DEV, LEAF_DEV), 1)
    above = lax.broadcasted_iota(jnp.int32, (NEAR, NEAR), 1)
    above = above < lax.broadcasted_iota(jnp.int32, (NEAR, NEAR), 0)

    def ranks(mask):
        flag = jnp.where(mask, 1.0, 0.0)
        line = jnp.broadcast_to(jnp.sum(flag, axis=1, keepdims=True), shape)
        rank = dot(flag.astype(BF), jnp.where(before, 1.0, 0.0).astype(BF))
        rank += dot(jnp.where(above, 1.0, 0.0).astype(BF), line.astype(BF))
        return rank, jnp.sum(jnp.sum(flag, axis=1, keepdims=True), axis=0, keepdims=True)

    rank_local, n_local = ranks(local)
    rank_other, n_other = ranks(live & ~local)
    rank = jnp.where(local, rank_local, jnp.where(live, rank_other + n_local, -1.0))
    rank = jnp.concatenate([rank, jnp.zeros((NEAR, 128 - LEAF_DEV), F32)], axis=1).T
    slot = lax.broadcasted_iota(jnp.int32, (LEAF_DEV, PAIRS), 1).astype(F32)
    row = lax.broadcasted_iota(jnp.int32, shape, 0)
    leaf = lax.broadcasted_iota(jnp.int32, shape, 1).astype(F32)
    known = jnp.where(live, partner, 0).astype(F32)
    found = jnp.zeros((NEAR, PAIRS), F32)
    for m in range(NEAR):
        hit = jnp.where(rank[:LEAF_DEV, m : m + 1] == slot, 1.0, 0.0).astype(BF)
        what = jnp.where(row == 0, known[m : m + 1], jnp.where(row == 1, leaf, 1.0))
        found += dot(what.astype(BF), hit)
    code = jnp.where(found[2:3] > 0.5, found[0:1] * LEAF_DEV + found[1:2], 3.0 * LEAF_DEV**2)
    at = lax.broadcasted_iota(jnp.int32, code.shape, 1)
    code = jnp.where(at == PAIRS - 2, n_local, code)
    return jnp.where(at == PAIRS - 1, n_local + n_other, code).astype(jnp.int32)


def up_kernel(
    where,
    lists_in,
    counts_in,
    vec_in,
    coords_in,
    basis_in,
    transfer_in,
    sk,
    dev,
    ee,
    xs,
    wide,
    pairs,
    lists,
    counts,
    coords,
    basis,
    transfer,
    tiles,
    nat,
    sem,
):
    copies = [
        pltpu.make_async_copy(transfer_in, transfer, sem.at[0]),
        pltpu.make_async_copy(vec_in, wide.at[pl.ds(0, VECS)], sem.at[1]),
        pltpu.make_async_copy(basis_in, basis, sem.at[2]),
        pltpu.make_async_copy(coords_in, coords, sem.at[3]),
        pltpu.make_async_copy(lists_in, lists, sem.at[4]),
        pltpu.make_async_copy(counts_in, counts, sem.at[5]),
    ]
    for c in copies:
        c.start()
    order = order_matrix(False)
    copies[0].wait()

    def group(g, _):
        base = pl.multiple_of(g * 16, 16)

        def write(m, child, value):
            ee[g * 8 + m, pl.ds(child * RANK, RANK), :] = value

        pack_transfer(
            lambda i: transfer[pl.ds(base, 16), pl.ds(i * 128, 128)], tiles, order, write
        )
        return 0

    lax.fori_loop(0, 4, group, 0)
    copies[1].wait()
    for c in copies[3:]:
        c.wait()
    pairs[...] = pair_list(lists[...], counts[...], (where[0] - 1) * LEAF_DEV)
    for i in range(LEAF_DEV):
        lanes = slice(i * LEAF, (i + 1) * LEAF)
        xs[i] = pieces(wide[0:VECS, lanes])
        c = coords[:, lanes]
        blank = jnp.zeros((1, LEAF), F32)
        wide[VECS : VECS + 8, lanes] = jnp.concatenate([c, blank, c, blank], axis=0)
    copies[2].wait()
    for m in range(LEAF_DEV // 2):
        x = xs[2 * m : 2 * m + 2].reshape(64, LEAF)
        b = basis[2 * m : 2 * m + 2].reshape(128, LEAF)
        r = dot(x, b, NT)
        nat[m] = joined(folded(r[:32]), folded(r[32:]))
    for m in range(LEAF_DEV // 2):
        sk[16 + m] = folded(dot(pieces(nat[m]), order))
    half = LEAF_DEV // 2
    while half > 1:
        for m in range(half, 2 * half, 2):
            a = folded(dot(pieces(sk[m]), ee[m]))
            b = folded(dot(pieces(sk[m + 1]), ee[m + 1]))
            sk[m // 2] = joined(a, b)
        half = half // 2
    top = folded(dot(pieces(sk[1]), ee[1]))
    sk[0] = jnp.where(low_lanes(top.shape), 0.0, top)
    dev[...] = joined(swapped(top[:8]), top[8:])
    for m in range(LEAF_DEV):
        for h in range(2):
            lanes = slice((2 * m + h) * 128, (2 * m + h + 1) * 128)
            wide[24:32, lanes] = sk[m, 8 * h : 8 * h + 8]


def split3(v):
    h1 = v.astype(BF).astype(F32)
    h2 = (v - h1).astype(BF).astype(F32)
    return h1, h2, (v - h1 - h2).astype(BF).astype(F32)


def features(c):
    row = lax.broadcasted_iota(jnp.int32, c.shape, 0)
    low = row < 4
    s = jnp.where(row % 4 < 3, (c - 0.5) * SIGMA, 0.0)
    h1, h2, h3 = split3(s)
    size = jnp.sum(jnp.where(low, s * s, 0.0), axis=0, keepdims=True)
    n1, n2, n3 = split3(size)
    j1, j2, j3 = split3(size + JITTER_SQ * SIGMA * SIGMA)

    def rows(*values):
        x = jnp.zeros(c.shape, F32)
        for at, v in enumerate(values):
            x = jnp.where(row == at, v, x)
        return x

    cross = -2.0 * jnp.where(low, h1, h2)
    own = [cross, cross, -2.0 * jnp.where(low, h3, h1), rows(j1, j2, j3, 1.0, 1.0, 1.0)]
    partner = [h1, h2, jnp.where(low, h1, h3), rows(1.0, 1.0, 1.0, n1, n2, n3)]
    return jnp.concatenate(own, axis=0), jnp.concatenate(partner, axis=0)


def four_leaves(c):
    own, partner = features(c)
    parts = [partner[:, q * LEAF : (q + 1) * LEAF] for q in range(4)]
    return own.astype(BF), jnp.concatenate(parts, axis=0).T.astype(BF)


def own_kernel(wide, partner, own):
    def prepare(i, _):
        lanes = pl.ds(pl.multiple_of(i * 4 * LEAF, 4 * LEAF), 4 * LEAF)
        mine, partner[i] = four_leaves(wide[VECS : VECS + 8, lanes])
        for q in range(4):
            own[4 * i + q, 0:96] = jnp.zeros((96, LEAF), BF)
            own[4 * i + q, 96:128] = mine[:, q * LEAF : (q + 1) * LEAF]
            own[4 * i + q, 128:224] = jnp.zeros((96, LEAF), BF)
        return 0

    lax.fori_loop(0, LEAF_DEV // 4, prepare, 0)


def other_kernel(xs_own, partner_own, before, after, xs, partner):
    xs[pl.ds(LEAF_DEV, LEAF_DEV)] = xs_own[...]
    xs[3 * LEAF_DEV] = jnp.zeros((32, LEAF), BF)
    partner[pl.ds(LEAF_DEV // 4, LEAF_DEV // 4)] = partner_own[...]
    partner[3 * LEAF_DEV // 4] = partner_own[0]

    def prepare(i, _):
        for at, wide in ((0, before), (2, after)):
            for q in range(4):
                lanes = pl.ds(pl.multiple_of((4 * i + q) * LEAF, LEAF), LEAF)
                xs[at * LEAF_DEV + 4 * i + q] = pieces(wide[0:VECS, lanes])
            lanes = pl.ds(pl.multiple_of(i * 4 * LEAF, 4 * LEAF), 4 * LEAF)
            _, partner[at * LEAF_DEV // 4 + i] = four_leaves(wide[VECS : VECS + 8, lanes])
        return 0

    lax.fori_loop(0, LEAF_DEV // 4, prepare, 0, unroll=2)


def near_kernel(chunk, pairs, xs, partner, own, *rest):
    out = rest[-1]
    start = lax.div(pairs[0, PAIRS - 2], GROUP)
    if chunk == 0:
        out[...] = jnp.zeros_like(out)
        begin, end, skip = 0, start, LEAF_DEV
    else:
        out[...] = rest[0][...]
        begin, end, skip = start, lax.div(pairs[0, PAIRS - 1] + GROUP - 1, GROUP), 0

    def step(i, _):
        for g in range(GROUP):
            code = pairs[0, i * GROUP + g]
            p = (code >> 5) - skip
            c = code & (LEAF_DEV - 1)
            rows = pl.ds(pl.multiple_of(96 - (p & 3) * 32, 32), 128)
            t = dot(partner[p >> 2], own[c, rows, :])
            u = t * lax.rsqrt(t)
            k = (u + LOG2E) * jnp.exp2(-u)
            khi = k.astype(BF)
            klo = (k - khi.astype(F32)).astype(BF)
            x = xs[p]
            r = folded(dot(x, khi)) + dot(x[:VECS], klo)
            lanes = pl.ds(pl.multiple_of(c * LEAF, LEAF), LEAF)
            out[:, lanes] = out[:, lanes] + r
        return 0

    lax.fori_loop(begin, end, step, 0)


def top_kernel(lists, where, tiles_in, ee_low, ee_high, coupling, out, q, blocks, raw, sem):
    d = where[0]
    devices = DEVICES
    levels = devices.bit_length() - 1
    order = order_matrix(False)
    nodes = [(devices + d) >> (levels - level) for level in range(levels + 1)]
    copies = [
        pltpu.make_async_copy(coupling.at[nodes[level]], raw.at[level], sem.at[level])
        for level in range(1, levels + 1)
    ]
    for c in copies:
        c.start()
    core, z, x, y = d & 1, (d >> 1) & 3, (d >> 3) & 3, (d >> 5) & 3

    def place(j, _):
        base = 4 * (((j & 3) - x) & 3) + 16 * (((j >> 2) - y) & 3)
        for u in range(4):
            at = base + ((u - z) & 3)
            a = tiles_in[at + 64 * core]
            b = tiles_in[at + 64 - 64 * core]
            m = 4 * j + u
            q[devices // 2 + m, 0:8] = joined(a, swapped(b))
            q[devices // 2 + m, 8:16] = joined(swapped(a), b)
        return 0

    lax.fori_loop(0, devices // 8, place, 0)

    def matrix(m, half):
        return ee_high[m - devices // 2] if half == devices // 2 else ee_low[m]

    half = devices // 2

    def parents(m, half):
        a = folded(dot(pieces(q[m]), matrix(m, half)))
        b = folded(dot(pieces(q[m + 1]), matrix(m + 1, half)))
        return joined(a, b)

    while half >= 2:
        if half >= 16:

            def some(i, _, half=half):
                for u in range(4):
                    m = half + 8 * i + 2 * u
                    q[m // 2] = parents(m, half)
                return 0

            lax.fori_loop(0, half // 8, some, 0)
        else:
            for m in range(half, 2 * half, 2):
                q[m // 2] = parents(m, half)
        half = half // 2
    for c in copies:
        c.wait()
    own = []
    for level in range(1, levels + 1):
        a = nodes[level]
        x = raw[level].astype(F32)
        for i in range(ROWS):
            blocks[pl.ds(i * 8, 2), :] = x[:, i * 128 : (i + 1) * 128]
        rhs, lhs = [], []
        for k in range(2):
            c = blocks[pl.ds(k, ROWS, stride=8), :]
            rhs += [c, swapped(c)]
            slot = lists[k, a]
            v = q[slot // 2]
            lhs.append(jnp.where(slot % 2 == k, v, swapped(v)))
        r = dot(pieces(joined(*lhs)), jnp.concatenate(rhs, axis=0).astype(BF))
        r = folded(dot(pieces(folded(r)), order))
        odd = a % 2 == 1
        r = jnp.where(odd, swapped(r), r)
        own.append(jnp.where(low_lanes(r.shape) != odd, r, 0.0))
    path = own[0]
    for level in range(2, levels + 1):
        r = folded(dot(pieces(path), matrix(nodes[level - 1], 1 << level - 1), NT))
        odd = nodes[level] % 2 == 1
        path = jnp.where(low_lanes(r.shape) != odd, r, 0.0) + own[level - 1]
    out[...] = jnp.where(nodes[levels] % 2 == 1, path, swapped(path))


def down_kernel(
    lists, where, sk_own, before, after, blocks, ee, basis, path, near, out, table, nat, field
):
    slots = 2 * LEAF_DEV
    first = (where[0] - 1) * slots
    order = order_matrix(False)
    back = order_matrix(True)

    def double(m, _):
        lanes = pl.ds(pl.multiple_of(m * 256, 256), 256)
        for at, wide in enumerate((before, None, after)):
            if wide is None:
                x = sk_own[m]
            else:
                x = wide[24:32, lanes]
                x = jnp.concatenate([x[:, :128], x[:, 128:]], axis=0)
            y = swapped(x)
            table[at * slots + 2 * m] = pieces(joined(x, y))
            table[at * slots + 2 * m + 1] = pieces(joined(y, x))
        return 0

    lax.fori_loop(0, LEAF_DEV, double, 0, unroll=2)

    def couple(i, _):
        for u in range(4):
            m = jnp.maximum(4 * i + u, 1)
            sides = []
            for side in range(2):
                j = 2 * m + side
                parts = []
                for k in range(0, FAR, 2):
                    a = table[lists[k, j] - first]
                    b = table[lists[k + 1, j] - first]
                    parts.append(joined(a, b))
                sides.append(folded(dot(jnp.concatenate(parts, axis=1), blocks[j])))
            nat[m] = joined(*sides)
        return 0

    nat[0] = jnp.zeros((VECS, 128), F32)
    lax.fori_loop(0, LEAF_DEV // 4, couple, 0)
    for i in range(LEAF_DEV // 8):
        x = nat[8 * i : 8 * i + 8].reshape(8 * VECS, 128)
        x = folded(dot(pieces(x), order))
        field[8 * i : 8 * i + 8] = x.reshape(8, VECS, 128)
    field[0] = path[...]
    for m in range(1, LEAF_DEV):
        x = field[m // 2]
        x = jnp.where(low_lanes(x.shape) != (m % 2 == 1), x, 0.0)
        field[m] = field[m] + folded(dot(pieces(x), ee[m], NT))
    for m in range(LEAF_DEV // 2):
        x = folded(dot(pieces(field[LEAF_DEV // 2 + m]), back))
        low = low_lanes(x.shape)
        lhs = jnp.concatenate(
            [pieces(jnp.where(low, x, 0.0)), pieces(jnp.where(low, 0.0, x))], axis=0
        )
        r = dot(lhs, basis[2 * m : 2 * m + 2].reshape(128, LEAF))
        for side in range(2):
            lanes = slice((2 * m + side) * LEAF, (2 * m + side + 1) * LEAF)
            far = folded(r[32 * side : 32 * side + 32])
            out[:, lanes] = far + near[:, lanes] * (LN2 / math.sqrt(LEAF))


def call(kernel, out_shape, in_specs, scratch=(), name=None, us=1, mib=16):
    return pl.pallas_call(
        kernel,
        out_shape=out_shape,
        in_specs=in_specs,
        out_specs=jax.tree.map(lambda _: VMEM, out_shape),
        scratch_shapes=list(scratch),
        compiler_params=pltpu.CompilerParams(vmem_limit_bytes=mib << 20),
        name=name,
        cost_estimate=pl.CostEstimate(
            flops=us * 10**9, bytes_accessed=us * 10**6, transcendentals=0
        ),
    )


def shaped(shape, dtype=F32):
    return jax.ShapeDtypeStruct(shape, dtype)


PHASES = ((2, 4), (8, 4), (32, 4), (1, 2))


def exchanged(tile, stride, size, devices):
    got = [tile]
    for k in range(1, size):
        pairs = []
        for i in range(devices):
            at = i // stride % size
            pairs.append((i, i + ((at - k) % size - at) * stride))
        got.append(lax.ppermute(tile, AXES, pairs))
    return got


def per_device(
    vectors,
    coords,
    leaf_basis,
    transfer,
    coupling,
    near_list,
    near_count,
    local_list,
    top_transfer,
    top_coupling,
    top_list,
):
    devices = lax.axis_size(AXES)
    position = lax.axis_index(AXES).astype(jnp.int32)
    where = position.reshape(1)
    up = [(i, i + 1) for i in range(devices - 1)]
    down = [(j, i) for i, j in up]
    sk, dev, ee, xs_own, wide, pairs = call(
        up_kernel,
        (
            shaped((LEAF_DEV, VECS, 128)),
            shaped((8, 128)),
            shaped((LEAF_DEV, 128, 128), BF),
            shaped((LEAF_DEV, 32, LEAF), BF),
            shaped((32, LEAF_DEV * LEAF)),
            shaped((1, PAIRS), jnp.int32),
        ),
        [SMEM] + [HBM] * 6,
        [
            pltpu.VMEM((NEAR, LEAF_DEV), jnp.int32),
            pltpu.VMEM((1, LEAF_DEV), jnp.int32),
            pltpu.VMEM((3, LEAF_DEV * LEAF), F32),
            pltpu.VMEM((LEAF_DEV, RANK, LEAF), BF),
            pltpu.VMEM((2 * LEAF_DEV, RANK * RANK), BF),
            pltpu.VMEM((2, PITCH * ROWS, 128), F32),
            pltpu.VMEM((16, VECS, 128), F32),
            pltpu.SemaphoreType.DMA((6,)),
        ],
        "up",
    )(
        where,
        *(
            pltpu.with_memory_space_constraint(x, pltpu.HBM)
            for x in (
                near_list.T,
                near_count.reshape(1, LEAF_DEV),
                vectors,
                coords,
                leaf_basis,
                transfer,
            )
        ),
    )
    order_scratch = [pltpu.VMEM((2, PITCH * ROWS, 128), F32)]

    def pack(x, first, name):
        return call(
            functools.partial(pack_kernel, first),
            shaped((devices // 2, 128, 128), BF),
            [VMEM],
            order_scratch,
            name,
            us=3,
        )(x)

    tied = lax.optimization_barrier
    got = exchanged(dev[None], *PHASES[0], devices)
    upper, _ = tied((top_transfer, dev))
    ee_low = pack(upper, 0, "pack0")
    *got, ee_low = tied((*got, ee_low))
    tiles = jnp.concatenate(got, axis=0)
    got = exchanged(tiles, *PHASES[1], devices)
    upper, _ = tied((top_transfer, tiles))
    ee_high = pack(upper, devices, "pack1")
    *got, ee_high = tied((*got, ee_high))
    tiles = jnp.concatenate(got, axis=0)
    got = exchanged(tiles, *PHASES[2], devices)
    stored, _ = tied((coupling, tiles))
    blocks = call(
        blocks_kernel,
        shaped((2 * LEAF_DEV, FAR * RANK, 128), BF),
        [VMEM],
        order_scratch,
        "blocks",
        us=3,
    )(jnp.transpose(stored, (1, 0, 2)))
    *got, blocks = tied((*got, blocks))
    tiles = jnp.concatenate(got, axis=0)
    got = exchanged(tiles, *PHASES[3], devices)
    wide_up, _ = tied((wide, tiles))
    before = lax.ppermute(wide_up, AXES, up)
    partner_own, own = call(
        own_kernel,
        (
            shaped((LEAF_DEV // 4, LEAF, 128), BF),
            shaped((LEAF_DEV, 224, LEAF), BF),
        ),
        [VMEM],
        (),
        "own",
        us=2,
    )(wide_up)
    *got, own = tied((*got, own))
    tiles = jnp.concatenate(got, axis=0)
    wide_down, _ = tied((wide, tiles))
    after = lax.ppermute(wide_down, AXES, down)
    levels = devices.bit_length() - 1
    path = call(
        top_kernel,
        shaped((VECS, 128)),
        [SMEM] * 2 + [VMEM] * 3 + [HBM],
        [
            pltpu.VMEM((devices, VECS, 128), F32),
            pltpu.VMEM((256, 128), F32),
            pltpu.VMEM((levels + 1, 2, RANK * RANK), BF),
            pltpu.SemaphoreType.DMA((levels + 1,)),
        ],
        "top",
        us=6,
    )(
        top_list.T,
        where,
        tiles,
        ee_low,
        ee_high,
        pltpu.with_memory_space_constraint(top_coupling, pltpu.HBM),
    )
    near = call(
        functools.partial(near_kernel, 0),
        shaped((VECS, LEAF_DEV * LEAF)),
        [SMEM] + [VMEM] * 3,
        (),
        "near0",
        us=8,
    )(pairs, xs_own, partner_own, own)
    near, before, after, path = tied((near, before, after, path))
    xs, partner = call(
        other_kernel,
        (
            shaped((3 * LEAF_DEV + 1, 32, LEAF), BF),
            shaped((3 * LEAF_DEV // 4 + 1, LEAF, 128), BF),
        ),
        [VMEM] * 4,
        (),
        "other",
        us=2,
    )(xs_own, partner_own, before, after)
    near = call(
        functools.partial(near_kernel, 1),
        shaped((VECS, LEAF_DEV * LEAF)),
        [SMEM] + [VMEM] * 4,
        (),
        "near1",
        us=8,
    )(pairs, xs, partner, own, near)
    return call(
        down_kernel,
        shaped((VECS, LEAF_DEV * LEAF)),
        [SMEM] * 2 + [VMEM] * 8,
        [
            pltpu.VMEM((6 * LEAF_DEV, 32, 128), BF),
            pltpu.VMEM((LEAF_DEV, VECS, 128), F32),
            pltpu.VMEM((LEAF_DEV, VECS, 128), F32),
        ],
        "down",
    )(local_list.T, where, sk, before, after, blocks, ee, leaf_basis, path, near)


def solution(mesh):
    split = P(None, AXES)
    return jax.shard_map(
        per_device,
        mesh=mesh,
        in_specs=(
            split,
            split,
            P(AXES, None, None),
            P(AXES, None),
            P(AXES, None, None),
            P(AXES, None),
            P(AXES),
            P(AXES, None),
            P(),
            P(),
            P(),
        ),
        out_specs=split,
        check_vma=False,
    )
```

profile of v0, /device:TPU:17, one launch (start us, length us, event | category | flops | bytes accessed | tf_op | source)
XLA Modules:
  0.0 75.1 jit_solution(6087178283838398858)
XLA Ops:
  0.0 4.2 %up.1 = (f32[32,16,128]{2,1,0:T(8,128)S(1)}, f32[8,128]{1,0:T(8,128)S(1)}, bf16[32,128,128]{2,1,0:T(8,128)(2,1)S(1)}, bf16[32,32,256]{2,1,0:T(8,128)(2,1)S(1)}, ...) custom-call(s32[1]{0:T(128)} %bitcast.1.where, s32[8,32]{1,0:T(8,128)} %bitcast.14, s32[1,32]{1,0:T(1,128)} %bitcast.15, ...), custom_call_target="tpu_custom_call" | custom-call | flops 1000000000 | bytes 1000000 | tf_op jit(solution)/shard_map/up/pallas_call | solution.py:533
  4.2 3.8 %collective-permute-start = (f32[1,8,128]{2,1,0:T(8,128)S(1)}, f32[1,8,128]{2,1,0:T(8,128)S(1)}, u32[]{:S(2)}, u32[]{:S(2)}) collective-permute-start(f32[1,8,128]{2,1,0:T(8,128)S(1)} %bitcast.8), channel_id=1, source_target_pairs={{0,6},{1,7},{2,0},{3,1},{4,2},{5,3},{6,4},{7,5},{8,14},{9,15},{10,... | collective-permute-start | bytes 12296 | tf_op jit(solution)/shard_map/ppermute | solution.py:511
  8.0 0.7 collective-permute-start.2
  8.7 2.1 %pack0.1.ee_low = bf16[64,128,128]{2,1,0:T(8,128)(2,1)S(1)} custom-call(bf16[256,4096]{1,0:T(8,128)(2,1)S(1)} %copy-done.3), custom_call_target="tpu_custom_call" | custom-call | flops 3000000000 | bytes 3000000 | tf_op jit(solution)/shard_map/pack0/pallas_call | solution.py:572
  10.8 0.0 collective-permute-done
  10.8 1.1 %collective-permute-done.1 = f32[1,8,128]{2,1,0:T(8,128)S(1)} collective-permute-done((f32[1,8,128]{2,1,0:T(8,128)S(1)}, f32[1,8,128]{2,1,0:T(8,128)S(1)}, u32[]{:S(2)}, u32[]{:S(2)}) %collective-permute-start.1) | collective-permute-done | bytes 4128 | tf_op jit(solution)/shard_map/ppermute | solution.py:511
  12.0 0.0 collective-permute-done.2
  12.0 0.0 copy-start.2
  12.0 2.5 %collective-permute-start.3 = (f32[4,8,128]{2,1,0:T(8,128)S(1)}, f32[4,8,128]{2,1,0:T(8,128)S(1)}, u32[]{:S(2)}, u32[]{:S(2)}) collective-permute-start(f32[4,8,128]{2,1,0:T(8,128)S(1)} %constant_dynamic-update-slice_fusion), channel_id=1, source_target_pairs={{0,24},{1,25},{2,26},{3,27},{4,28},{5,29},{6,30},{7,31},{8,0},{9,1... | collective-permute-start | bytes 49160 | tf_op jit(solution)/shard_map/ppermute | solution.py:511
  14.5 0.5 collective-permute-start.4
  15.1 0.6 collective-permute-start.5
  15.7 2.1 %pack1.1.ee_high = bf16[64,128,128]{2,1,0:T(8,128)(2,1)S(1)} custom-call(bf16[256,4096]{1,0:T(8,128)(2,1)S(1)} %copy-done.3), custom_call_target="tpu_custom_call" | custom-call | flops 3000000000 | bytes 3000000 | tf_op jit(solution)/shard_map/pack1/pallas_call | solution.py:572
  17.8 0.8 %collective-permute-done.4 = f32[4,8,128]{2,1,0:T(8,128)S(1)} collective-permute-done((f32[4,8,128]{2,1,0:T(8,128)S(1)}, f32[4,8,128]{2,1,0:T(8,128)S(1)}, u32[]{:S(2)}, u32[]{:S(2)}) %collective-permute-start.4) | collective-permute-done | bytes 16416 | tf_op jit(solution)/shard_map/ppermute | solution.py:511
  18.6 0.2 collective-permute-done.5
  18.9 0.2 collective-permute-start.6
  19.1 2.6 %collective-permute-start.7 = (f32[16,8,128]{2,1,0:T(8,128)S(1)}, f32[16,8,128]{2,1,0:T(8,128)S(1)}, u32[]{:S(2)}, u32[]{:S(2)}) collective-permute-start(f32[16,8,128]{2,1,0:T(8,128)S(1)} %constant_dynamic-update-slice_fusion.4), channel_id=1, source_target_pairs={{0,64},{1,65},{2,66},{3,67},{4,68},{5,69},{6,70},{7,71},{8,72},{9,... | collective-permute-start | bytes 196616 | tf_op jit(solution)/shard_map/ppermute | solution.py:511
  21.8 3.0 %blocks.1 = bf16[64,384,128]{2,1,0:T(8,128)(2,1)S(1)} custom-call(bf16[6,64,4096]{2,1,0:T(8,128)(2,1)S(1)} %bitcast.12), custom_call_target="tpu_custom_call" | custom-call | flops 3000000000 | bytes 3000000 | tf_op jit(solution)/shard_map/blocks/pallas_call | solution.py:594
  24.7 0.0 collective-permute-done.7
  24.8 0.1 collective-permute-done.8
  24.9 5.6 %collective-permute-start.9 = (f32[64,8,128]{2,1,0:T(8,128)S(1)}, f32[64,8,128]{2,1,0:T(8,128)S(1)}, u32[]{:S(2)}, u32[]{:S(2)}) collective-permute-start(f32[64,8,128]{2,1,0:T(8,128)S(1)} %constant_dynamic-update-slice_fusion.8), channel_id=1, source_target_pairs={{0,1},{1,0},{2,3},{3,2},{4,5},{5,4},{6,7},{7,6},{8,9},{9,8},{10,11... | collective-permute-start | bytes 786440 | tf_op jit(solution)/shard_map/ppermute | solution.py:511
  30.5 2.1 %collective-permute-start.10 = (f32[32,8192]{1,0:T(8,128)S(1)}, f32[32,8192]{1,0:T(8,128)S(1)}, u32[]{:S(2)}, u32[]{:S(2)}) collective-permute-start(f32[32,8192]{1,0:T(8,128)S(1)} %get-tuple-element.68.wide), channel_id=1, source_target_pairs={{0,1},{1,2},{2,3},{3,4},{4,5},{5,6},{6,7},{7,8},{8,9},{9,10},{10,1... | collective-permute-start | bytes 3145736 | tf_op jit(solution)/shard_map/ppermute | solution.py:606
  32.6 1.1 %own.1 = (bf16[8,256,128]{2,1,0:T(8,128)(2,1)S(1)}, bf16[32,224,256]{2,1,0:T(8,128)(2,1)S(1)}) custom-call(f32[32,8192]{1,0:T(8,128)S(1)} %get-tuple-element.68.wide), custom_call_target="tpu_custom_call" | custom-call | flops 2000000000 | bytes 2000000 | tf_op jit(solution)/shard_map/own/pallas_call | solution.py:607
  33.7 0.0 collective-permute-done.9
  33.8 2.4 %collective-permute-start.11 = (f32[32,8192]{1,0:T(8,128)S(1)}, f32[32,8192]{1,0:T(8,128)S(1)}, u32[]{:S(2)}, u32[]{:S(2)}) collective-permute-start(f32[32,8192]{1,0:T(8,128)S(1)} %get-tuple-element.68.wide), channel_id=1, source_target_pairs={{1,0},{2,1},{3,2},{4,3},{5,4},{6,5},{7,6},{8,7},{9,8},{10,9},{11,1... | collective-permute-start | bytes 3145736 | tf_op jit(solution)/shard_map/ppermute | solution.py:621
  36.2 10.6 %top.1.path = f32[16,128]{1,0:T(8,128)S(1)} custom-call(s32[2,256]{1,0:T(2,128)S(1)} %bitcast.13, s32[1]{0:T(128)} %bitcast.1.where, f32[128,8,128]{2,1,0:T(8,128)S(1)} %constant_dynamic-update-slice_fusion.12.tiles_in, bf16[64,128,128]{2,1,0:T(8,128)(2,1)S(1)} %pack0.1.ee_low, bf16[64,128,128]{2,1,0:T(8,128)(2,1)S(1)} %pack1.1.ee_high, ...), custom_call_target="tpu_custom_call" | custom-call | flops 6000000000 | bytes 6000000 | tf_op jit(solution)/shard_map/top/pallas_call | solution.py:623
  46.7 8.5 %near0.1.rest_0_ = f32[16,8192]{1,0:T(8,128)S(1)} custom-call(s32[1,384]{1,0:T(1,128)S(1)} %get-tuple-element.43.pairs, bf16[32,32,256]{2,1,0:T(8,128)(2,1)S(1)} %get-tuple-element.44.xs.xs_own, bf16[8,256,128]{2,1,0:T(8,128)(2,1)S(1)} %get-tuple-element.63.partner.partner_own, bf16[32,224,256]{2,1,0:T(8,128)(2,1)S(1)} %get-tuple-element.65.own), custom_call_target="tpu_custom_call" | custom-call | flops 8000000000 | bytes 8000000 | tf_op jit(solution)/shard_map/near0/pallas_call | solution.py:643
  55.2 0.0 collective-permute-done.11.after
  55.2 1.0 %other.1 = (bf16[97,32,256]{2,1,0:T(8,128)(2,1)S(1)}, bf16[25,256,128]{2,1,0:T(8,128)(2,1)S(1)}) custom-call(bf16[32,32,256]{2,1,0:T(8,128)(2,1)S(1)} %get-tuple-element.44.xs.xs_own, bf16[8,256,128]{2,1,0:T(8,128)(2,1)S(1)} %get-tuple-element.63.partner.partner_own, f32[32,8192]{1,0:T(8,128)S(1)} %collective-permute-done.10.before, ...), custom_call_target="tpu_custom_call" | custom-call | flops 2000000000 | bytes 2000000 | tf_op jit(solution)/shard_map/other/pallas_call | solution.py:652
  56.3 0.0 copy-start
  56.3 0.0 copy-start.1
  56.3 12.4 %near1.1.near = f32[16,8192]{1,0:T(8,128)S(1)} custom-call(s32[1,384]{1,0:T(1,128)S(1)} %get-tuple-element.43.pairs, bf16[97,32,256]{2,1,0:T(8,128)(2,1)S(1)} %get-tuple-element.76.xs, bf16[25,256,128]{2,1,0:T(8,128)(2,1)S(1)} %get-tuple-element.77.partner, bf16[32,224,256]{2,1,0:T(8,128)(2,1)S(1)} %get-tuple-element.65.own, f32[16,8192]{1,0:T(8,128)S(1)} %near0.1.rest_0_), custom_call_target="tpu_custom_call" | custom-call | flops 8000000000 | bytes 8000000 | tf_op jit(solution)/shard_map/near1/pallas_call | solution.py:663
  68.7 6.4 %down.1 = f32[16,8192]{1,0:T(8,128)} custom-call(s32[6,64]{1,0:T(8,128)S(1)} %bitcast.7, s32[1]{0:T(128)} %bitcast.1.where, f32[32,16,128]{2,1,0:T(8,128)S(1)} %get-tuple-element.42.sk_own, f32[32,8192]{1,0:T(8,128)S(1)} %collective-permute-done.10.before, f32[32,8192]{1,0:T(8,128)S(1)} %collective-permute-done.11.after, bf16[64,384,128]{2,1,0:T(8,128)(2,1)S(1)} %blocks.1, ...), custom_call_target="tpu_custom_call" | custom-call | flops 1000000000 | bytes 1000000 | tf_op jit(solution)/shard_map/down/pallas_call | solution.py:671
  (26 shorter events, 0.1 us)
Async XLA Ops:
  0.0 8.7 %copy-start.3 = (bf16[256,4096]{1,0:T(8,128)(2,1)S(1)}, bf16[256,4096]{1,0:T(8,128)(2,1)}, u32[]{:S(2)}) copy-start(bf16[256,4096]{1,0:T(8,128)(2,1)} %transfer.1) | copy-start | bytes 6291460
  4.2 6.6 %collective-permute-start = (f32[1,8,128]{2,1,0:T(8,128)S(1)}, f32[1,8,128]{2,1,0:T(8,128)S(1)}, u32[]{:S(2)}, u32[]{:S(2)}) collective-permute-start(f32[1,8,128]{2,1,0:T(8,128)S(1)} %bitcast.8), channel_id=1, source_target_pairs={{0,6},{1,7},{2,0},{3,1},{4,2},{5,3},{6,4},{7,5},{8,14},{9,15},{10,... | collective-permute-start | bytes 12296 | tf_op jit(solution)/shard_map/ppermute | solution.py:511
  8.0 4.0 %collective-permute-start.1 = (f32[1,8,128]{2,1,0:T(8,128)S(1)}, f32[1,8,128]{2,1,0:T(8,128)S(1)}, u32[]{:S(2)}, u32[]{:S(2)}) collective-permute-start(f32[1,8,128]{2,1,0:T(8,128)S(1)} %bitcast.9), channel_id=1, source_target_pairs={{0,4},{1,5},{2,6},{3,7},{4,0},{5,1},{6,2},{7,3},{8,12},{9,13},{10,... | collective-permute-start | bytes 12296 | tf_op jit(solution)/shard_map/ppermute | solution.py:511
  8.0 4.0 %collective-permute-start.2 = (f32[1,8,128]{2,1,0:T(8,128)S(1)}, f32[1,8,128]{2,1,0:T(8,128)S(1)}, u32[]{:S(2)}, u32[]{:S(2)}) collective-permute-start(f32[1,8,128]{2,1,0:T(8,128)S(1)} %bitcast.10), channel_id=1, source_target_pairs={{0,2},{1,3},{2,4},{3,5},{4,6},{5,7},{6,0},{7,1},{8,10},{9,11},{10,... | collective-permute-start | bytes 12296 | tf_op jit(solution)/shard_map/ppermute | solution.py:511
  12.0 9.8 %copy-start.2 = (bf16[64,6,4096]{2,0,1:T(8,128)(2,1)S(1)}, bf16[64,6,4096]{2,0,1:T(8,128)(2,1)}, u32[]{:S(2)}) copy-start(bf16[64,6,4096]{2,0,1:T(8,128)(2,1)} %param.15) | copy-start | bytes 9437188
  12.0 5.8 %collective-permute-start.3 = (f32[4,8,128]{2,1,0:T(8,128)S(1)}, f32[4,8,128]{2,1,0:T(8,128)S(1)}, u32[]{:S(2)}, u32[]{:S(2)}) collective-permute-start(f32[4,8,128]{2,1,0:T(8,128)S(1)} %constant_dynamic-update-slice_fusion), channel_id=1, source_target_pairs={{0,24},{1,25},{2,26},{3,27},{4,28},{5,29},{6,30},{7,31},{8,0},{9,1... | collective-permute-start | bytes 49160 | tf_op jit(solution)/shard_map/ppermute | solution.py:511
  14.5 4.1 %collective-permute-start.4 = (f32[4,8,128]{2,1,0:T(8,128)S(1)}, f32[4,8,128]{2,1,0:T(8,128)S(1)}, u32[]{:S(2)}, u32[]{:S(2)}) collective-permute-start(f32[4,8,128]{2,1,0:T(8,128)S(1)} %constant_dynamic-update-slice_fusion), channel_id=1, source_target_pairs={{0,16},{1,17},{2,18},{3,19},{4,20},{5,21},{6,22},{7,23},{8,24},{9,... | collective-permute-start | bytes 49160 | tf_op jit(solution)/shard_map/ppermute | solution.py:511
  15.1 3.8 %collective-permute-start.5 = (f32[4,8,128]{2,1,0:T(8,128)S(1)}, f32[4,8,128]{2,1,0:T(8,128)S(1)}, u32[]{:S(2)}, u32[]{:S(2)}) collective-permute-start(f32[4,8,128]{2,1,0:T(8,128)S(1)} %constant_dynamic-update-slice_fusion), channel_id=1, source_target_pairs={{0,8},{1,9},{2,10},{3,11},{4,12},{5,13},{6,14},{7,15},{8,16},{9,17... | collective-permute-start | bytes 49160 | tf_op jit(solution)/shard_map/ppermute | solution.py:511
  18.9 5.9 %collective-permute-start.6 = (f32[16,8,128]{2,1,0:T(8,128)S(1)}, f32[16,8,128]{2,1,0:T(8,128)S(1)}, u32[]{:S(2)}, u32[]{:S(2)}) collective-permute-start(f32[16,8,128]{2,1,0:T(8,128)S(1)} %constant_dynamic-update-slice_fusion.4), channel_id=1, source_target_pairs={{0,96},{1,97},{2,98},{3,99},{4,100},{5,101},{6,102},{7,103},{8,104... | collective-permute-start | bytes 196616 | tf_op jit(solution)/shard_map/ppermute | solution.py:511
  19.1 5.6 %collective-permute-start.7 = (f32[16,8,128]{2,1,0:T(8,128)S(1)}, f32[16,8,128]{2,1,0:T(8,128)S(1)}, u32[]{:S(2)}, u32[]{:S(2)}) collective-permute-start(f32[16,8,128]{2,1,0:T(8,128)S(1)} %constant_dynamic-update-slice_fusion.4), channel_id=1, source_target_pairs={{0,64},{1,65},{2,66},{3,67},{4,68},{5,69},{6,70},{7,71},{8,72},{9,... | collective-permute-start | bytes 196616 | tf_op jit(solution)/shard_map/ppermute | solution.py:511
  21.7 3.1 %collective-permute-start.8 = (f32[16,8,128]{2,1,0:T(8,128)S(1)}, f32[16,8,128]{2,1,0:T(8,128)S(1)}, u32[]{:S(2)}, u32[]{:S(2)}) collective-permute-start(f32[16,8,128]{2,1,0:T(8,128)S(1)} %constant_dynamic-update-slice_fusion.4), channel_id=1, source_target_pairs={{0,32},{1,33},{2,34},{3,35},{4,36},{5,37},{6,38},{7,39},{8,40},{9,... | collective-permute-start | bytes 196616 | tf_op jit(solution)/shard_map/ppermute | solution.py:511
  24.9 8.8 %collective-permute-start.9 = (f32[64,8,128]{2,1,0:T(8,128)S(1)}, f32[64,8,128]{2,1,0:T(8,128)S(1)}, u32[]{:S(2)}, u32[]{:S(2)}) collective-permute-start(f32[64,8,128]{2,1,0:T(8,128)S(1)} %constant_dynamic-update-slice_fusion.8), channel_id=1, source_target_pairs={{0,1},{1,0},{2,3},{3,2},{4,5},{5,4},{6,7},{7,6},{8,9},{9,8},{10,11... | collective-permute-start | bytes 786440 | tf_op jit(solution)/shard_map/ppermute | solution.py:511
  30.5 5.6 %copy-start.4 = (s32[256,2]{0,1:T(2,128)S(1)}, s32[256,2]{0,1:T(2,128)}, u32[]{:S(2)}) copy-start(s32[256,2]{0,1:T(2,128)} %param.21) | copy-start | bytes 6148
  30.5 24.7 %collective-permute-start.10 = (f32[32,8192]{1,0:T(8,128)S(1)}, f32[32,8192]{1,0:T(8,128)S(1)}, u32[]{:S(2)}, u32[]{:S(2)}) collective-permute-start(f32[32,8192]{1,0:T(8,128)S(1)} %get-tuple-element.68.wide), channel_id=1, source_target_pairs={{0,1},{1,2},{2,3},{3,4},{4,5},{5,6},{6,7},{7,8},{8,9},{9,10},{10,1... | collective-permute-start | bytes 3145736 | tf_op jit(solution)/shard_map/ppermute | solution.py:606
  33.8 21.5 %collective-permute-start.11 = (f32[32,8192]{1,0:T(8,128)S(1)}, f32[32,8192]{1,0:T(8,128)S(1)}, u32[]{:S(2)}, u32[]{:S(2)}) collective-permute-start(f32[32,8192]{1,0:T(8,128)S(1)} %get-tuple-element.68.wide), channel_id=1, source_target_pairs={{1,0},{2,1},{3,2},{4,3},{5,4},{6,5},{7,6},{8,7},{9,8},{10,9},{11,1... | collective-permute-start | bytes 3145736 | tf_op jit(solution)/shard_map/ppermute | solution.py:621
  56.3 12.4 %copy-start = (bf16[32,64,256]{2,1,0:T(8,128)(2,1)S(1)}, bf16[32,64,256]{2,1,0:T(8,128)(2,1)}, u32[]{:S(2)}) copy-start(bf16[32,64,256]{2,1,0:T(8,128)(2,1)} %basis.1) | copy-start | bytes 3145732
  56.3 12.4 %copy-start.1 = (s32[64,6]{0,1:T(8,128)S(1)}, s32[64,6]{0,1:T(8,128)}, u32[]{:S(2)}) copy-start(s32[64,6]{0,1:T(8,128)} %param.18) | copy-start | bytes 4612
where the time goes:
time: 74.8 us; the launch traced here: 75.1 us
  Pallas kernels  51.3 us (69%)
  starting transfers between devices  21.1 us (28%)
  waiting for transfers between devices  2.34 us (3%)
    ppermute x10, starting transfers between devices, exchanged(): got.append(lax.ppermute(tile, AXES, pairs))  16.7 us
    pallas_call x1, Pallas kernels, per_device(): call(functools.partial(near_kernel, 1), shaped((VECS, LEAF_DEV * LEAF)),...  12.4 us
    pallas_call x1, Pallas kernels, per_device(): call(top_kernel, shaped((VECS, 128)), [SMEM] * 2 + [VMEM] * 3 + [HBM], [p...  10.6 us
    pallas_call x1, Pallas kernels, per_device(): call(functools.partial(near_kernel, 0), shaped((VECS, LEAF_DEV * LEAF)),...  8.49 us
    pallas_call x1, Pallas kernels, per_device(): call(down_kernel, shaped((VECS, LEAF_DEV * LEAF)), [SMEM] * 2 + [VMEM] *...  6.39 us
    pallas_call x2, Pallas kernels, pack(): call(functools.partial(pack_kernel, first), shaped((devices // 2, 128, 12...  4.19 us
    pallas_call x1, Pallas kernels, per_device(): call(up_kernel, (shaped((LEAF_DEV, VECS, 128)), shaped((8, 128)), shaped(...  4.16 us
    pallas_call x1, Pallas kernels, per_device(): call(blocks_kernel, shaped((2 * LEAF_DEV, FAR * RANK, 128), BF), [VMEM],...  2.98 us
  transfers between devices with their start and end apart: 12, of which 4 were waited for; matrix products, arithmetic and copies ran while one was open for 0% of the time, Pallas kernels for 36%

commit v1 on v0

--- a/solution.py
+++ b/solution.py
@@ -88,42 +88,51 @@
         write(s // 2, s % 2, jnp.concatenate(rows, axis=0).astype(BF))
 
 
-def pack_kernel(first, transfer, ee, tiles):
+def pack_kernel(transfer, ee, tiles):
     order = order_matrix(False)
 
-    def group(g, _):
-        base = pl.multiple_of(first + g * 16, 16)
-
-        def write(m, child, value):
-            ee[g * 8 + m, pl.ds(child * RANK, RANK), :] = value
-
-        pack_transfer(
-            lambda i: transfer[pl.ds(base, 16), pl.ds(i * 128, 128)], tiles, order, write
-        )
-        return 0
-
-    lax.fori_loop(0, transfer.shape[0] // 32, group, 0)
+    def groups(i, _):
+        for u in range(2):
+            g = 2 * i + u
+            base = pl.multiple_of(g * 16, 16)
+
+            def write(m, child, value, g=g):
+                ee[g * 8 + m, pl.ds(child * RANK, RANK), :] = value
+
+            pack_transfer(
+                lambda i, base=base: transfer[pl.ds(base, 16), pl.ds(i * 128, 128)],
+                tiles.at[u],
+                order,
+                write,
+            )
+        return 0
+
+    lax.fori_loop(0, transfer.shape[0] // 32, groups, 0)
 
 
 def blocks_kernel(coupling, blocks, tiles):
     for k in range(FAR):
 
-        def group(g, _):
-            base = pl.multiple_of(g * 16, 16)
-
-            def write(s, c):
-                y = swapped(c)
-                rows = [y, c] if s % 2 else [c, y]
-                blocks[g * 16 + s, k * RANK : (k + 1) * RANK, :] = jnp.concatenate(
-                    rows, axis=0
-                ).astype(BF)
-
-            unpack_rows(
-                lambda i: coupling[k, pl.ds(base, 16), pl.ds(i * 128, 128)], tiles, write
-            )
+        def groups(i, _):
+            for u in range(2):
+                g = 2 * i + u
+                base = pl.multiple_of(g * 16, 16)
+
+                def write(s, c, g=g):
+                    y = swapped(c)
+                    rows = [y, c] if s % 2 else [c, y]
+                    blocks[g * 16 + s, k * RANK : (k + 1) * RANK, :] = jnp.concatenate(
+                        rows, axis=0
+                    ).astype(BF)
+
+                unpack_rows(
+                    lambda i, base=base: coupling[k, pl.ds(base, 16), pl.ds(i * 128, 128)],
+                    tiles.at[u],
+                    write,
+                )
             return 0
 
-        lax.fori_loop(0, 2 * LEAF_DEV // 16, group, 0)
+        lax.fori_loop(0, 2 * LEAF_DEV // 32, groups, 0)
 
 
 def pair_list(lists, counts, first):
@@ -237,7 +246,7 @@
         half = half // 2
     top = folded(dot(pieces(sk[1]), ee[1]))
     sk[0] = jnp.where(low_lanes(top.shape), 0.0, top)
-    dev[...] = joined(swapped(top[:8]), top[8:])
+    dev[...] = jnp.broadcast_to(joined(swapped(top[:8]), top[8:])[None], dev.shape)
     for m in range(LEAF_DEV):
         for h in range(2):
             lanes = slice((2 * m + h) * 128, (2 * m + h + 1) * 128)
@@ -338,7 +347,7 @@
     lax.fori_loop(begin, end, step, 0)
 
 
-def top_kernel(lists, where, tiles_in, ee_low, ee_high, coupling, out, q, blocks, raw, sem):
+def top_kernel(lists, where, tiles_in, ee, coupling, out, q, blocks, raw, sem):
     d = where[0]
     devices = DEVICES
     levels = devices.bit_length() - 1
@@ -350,44 +359,36 @@
     ]
     for c in copies:
         c.start()
-    core, z, x, y = d & 1, (d >> 1) & 3, (d >> 3) & 3, (d >> 5) & 3
-
-    def place(j, _):
-        base = 4 * (((j & 3) - x) & 3) + 16 * (((j >> 2) - y) & 3)
-        for u in range(4):
-            at = base + ((u - z) & 3)
-            a = tiles_in[at + 64 * core]
-            b = tiles_in[at + 64 - 64 * core]
-            m = 4 * j + u
-            q[devices // 2 + m, 0:8] = joined(a, swapped(b))
-            q[devices // 2 + m, 8:16] = joined(swapped(a), b)
-        return 0
-
-    lax.fori_loop(0, devices // 8, place, 0)
-
-    def matrix(m, half):
-        return ee_high[m - devices // 2] if half == devices // 2 else ee_low[m]
+
+    def place(m, _):
+        a = tiles_in[2 * m]
+        b = tiles_in[2 * m + 1]
+        q[devices // 2 + m, 0:8] = joined(a, swapped(b))
+        q[devices // 2 + m, 8:16] = joined(swapped(a), b)
+        return 0
+
+    lax.fori_loop(0, devices // 2, place, 0, unroll=8)
 
     half = devices // 2
 
-    def parents(m, half):
-        a = folded(dot(pieces(q[m]), matrix(m, half)))
-        b = folded(dot(pieces(q[m + 1]), matrix(m + 1, half)))
+    def parents(m):
+        a = folded(dot(pieces(q[m]), ee[m]))
+        b = folded(dot(pieces(q[m + 1]), ee[m + 1]))
         return joined(a, b)
 
     while half >= 2:
-        if half >= 16:
+        if half >= 64:
 
             def some(i, _, half=half):
-                for u in range(4):
-                    m = half + 8 * i + 2 * u
-                    q[m // 2] = parents(m, half)
+                for u in range(16):
+                    m = half + 32 * i + 2 * u
+                    q[m // 2] = parents(m)
                 return 0
 
-            lax.fori_loop(0, half // 8, some, 0)
+            lax.fori_loop(0, half // 32, some, 0)
         else:
             for m in range(half, 2 * half, 2):
-                q[m // 2] = parents(m, half)
+                q[m // 2] = parents(m)
         half = half // 2
     for c in copies:
         c.wait()
@@ -411,7 +412,7 @@
         own.append(jnp.where(low_lanes(r.shape) != odd, r, 0.0))
     path = own[0]
     for level in range(2, levels + 1):
-        r = folded(dot(pieces(path), matrix(nodes[level - 1], 1 << level - 1), NT))
+        r = folded(dot(pieces(path), ee[nodes[level - 1]], NT))
         odd = nodes[level] % 2 == 1
         path = jnp.where(low_lanes(r.shape) != odd, r, 0.0) + own[level - 1]
     out[...] = jnp.where(nodes[levels] % 2 == 1, path, swapped(path))
@@ -441,8 +442,8 @@
     lax.fori_loop(0, LEAF_DEV, double, 0, unroll=2)
 
     def couple(i, _):
-        for u in range(4):
-            m = jnp.maximum(4 * i + u, 1)
+        for u in range(8):
+            m = jnp.maximum(8 * i + u, 1)
             sides = []
             for side in range(2):
                 j = 2 * m + side
@@ -456,7 +457,7 @@
         return 0
 
     nat[0] = jnp.zeros((VECS, 128), F32)
-    lax.fori_loop(0, LEAF_DEV // 4, couple, 0)
+    lax.fori_loop(0, LEAF_DEV // 8, couple, 0)
     for i in range(LEAF_DEV // 8):
         x = nat[8 * i : 8 * i + 8].reshape(8 * VECS, 128)
         x = folded(dot(pieces(x), order))
@@ -496,20 +497,6 @@
 
 def shaped(shape, dtype=F32):
     return jax.ShapeDtypeStruct(shape, dtype)
-
-
-PHASES = ((2, 4), (8, 4), (32, 4), (1, 2))
-
-
-def exchanged(tile, stride, size, devices):
-    got = [tile]
-    for k in range(1, size):
-        pairs = []
-        for i in range(devices):
-            at = i // stride % size
-            pairs.append((i, i + ((at - k) % size - at) * stride))
-        got.append(lax.ppermute(tile, AXES, pairs))
-    return got
 
 
 def per_device(
@@ -534,7 +521,7 @@
         up_kernel,
         (
             shaped((LEAF_DEV, VECS, 128)),
-            shaped((8, 128)),
+            shaped((DEVICES, 8, 128)),
             shaped((LEAF_DEV, 128, 128), BF),
             shaped((LEAF_DEV, 32, LEAF), BF),
             shaped((32, LEAF_DEV * LEAF)),
@@ -566,44 +553,11 @@
             )
         ),
     )
-    order_scratch = [pltpu.VMEM((2, PITCH * ROWS, 128), F32)]
-
-    def pack(x, first, name):
-        return call(
-            functools.partial(pack_kernel, first),
-            shaped((devices // 2, 128, 128), BF),
-            [VMEM],
-            order_scratch,
-            name,
-            us=3,
-        )(x)
-
+    order_scratch = [pltpu.VMEM((2, 2, PITCH * ROWS, 128), F32)]
     tied = lax.optimization_barrier
-    got = exchanged(dev[None], *PHASES[0], devices)
-    upper, _ = tied((top_transfer, dev))
-    ee_low = pack(upper, 0, "pack0")
-    *got, ee_low = tied((*got, ee_low))
-    tiles = jnp.concatenate(got, axis=0)
-    got = exchanged(tiles, *PHASES[1], devices)
-    upper, _ = tied((top_transfer, tiles))
-    ee_high = pack(upper, devices, "pack1")
-    *got, ee_high = tied((*got, ee_high))
-    tiles = jnp.concatenate(got, axis=0)
-    got = exchanged(tiles, *PHASES[2], devices)
-    stored, _ = tied((coupling, tiles))
-    blocks = call(
-        blocks_kernel,
-        shaped((2 * LEAF_DEV, FAR * RANK, 128), BF),
-        [VMEM],
-        order_scratch,
-        "blocks",
-        us=3,
-    )(jnp.transpose(stored, (1, 0, 2)))
-    *got, blocks = tied((*got, blocks))
-    tiles = jnp.concatenate(got, axis=0)
-    got = exchanged(tiles, *PHASES[3], devices)
-    wide_up, _ = tied((wide, tiles))
-    before = lax.ppermute(wide_up, AXES, up)
+    tiles = lax.all_to_all(dev, AXES, 0, 0, tiled=True)
+    before = lax.ppermute(wide, AXES, up)
+    after = lax.ppermute(wide, AXES, down)
     partner_own, own = call(
         own_kernel,
         (
@@ -614,32 +568,7 @@
         (),
         "own",
         us=2,
-    )(wide_up)
-    *got, own = tied((*got, own))
-    tiles = jnp.concatenate(got, axis=0)
-    wide_down, _ = tied((wide, tiles))
-    after = lax.ppermute(wide_down, AXES, down)
-    levels = devices.bit_length() - 1
-    path = call(
-        top_kernel,
-        shaped((VECS, 128)),
-        [SMEM] * 2 + [VMEM] * 3 + [HBM],
-        [
-            pltpu.VMEM((devices, VECS, 128), F32),
-            pltpu.VMEM((256, 128), F32),
-            pltpu.VMEM((levels + 1, 2, RANK * RANK), BF),
-            pltpu.SemaphoreType.DMA((levels + 1,)),
-        ],
-        "top",
-        us=6,
-    )(
-        top_list.T,
-        where,
-        tiles,
-        ee_low,
-        ee_high,
-        pltpu.with_memory_space_constraint(top_coupling, pltpu.HBM),
-    )
+    )(wide)
     near = call(
         functools.partial(near_kernel, 0),
         shaped((VECS, LEAF_DEV * LEAF)),
@@ -648,7 +577,7 @@
         "near0",
         us=8,
     )(pairs, xs_own, partner_own, own)
-    near, before, after, path = tied((near, before, after, path))
+    near, before, after = tied((near, before, after))
     xs, partner = call(
         other_kernel,
         (
@@ -668,6 +597,39 @@
         "near1",
         us=8,
     )(pairs, xs, partner, own, near)
+    tiles, near = tied((tiles, near))
+    upper, stored, _ = tied((top_transfer, coupling, tiles))
+    ee_top = call(
+        pack_kernel, shaped((devices, 128, 128), BF), [VMEM], order_scratch, "pack", us=4
+    )(upper)
+    levels = devices.bit_length() - 1
+    path = call(
+        top_kernel,
+        shaped((VECS, 128)),
+        [SMEM] * 2 + [VMEM] * 2 + [HBM],
+        [
+            pltpu.VMEM((devices, VECS, 128), F32),
+            pltpu.VMEM((256, 128), F32),
+            pltpu.VMEM((levels + 1, 2, RANK * RANK), BF),
+            pltpu.SemaphoreType.DMA((levels + 1,)),
+        ],
+        "top",
+        us=6,
+    )(
+        top_list.T,
+        where,
+        tiles,
+        ee_top,
+        pltpu.with_memory_space_constraint(top_coupling, pltpu.HBM),
+    )
+    blocks = call(
+        blocks_kernel,
+        shaped((2 * LEAF_DEV, FAR * RANK, 128), BF),
+        [VMEM],
+        order_scratch,
+        "blocks",
+        us=3,
+    )(jnp.transpose(stored, (1, 0, 2)))
     return call(
         down_kernel,
         shaped((VECS, LEAF_DEV * LEAF)),

time: 74.8 us -> 70.7 us (0.945)
  the two profiles are of different devices: /device:TPU:17 before, /device:TPU:0 now
where the time goes in v1:
time: 70.7 us; the launch traced here: 70 us
  Pallas kernels  45.1 us (64%)
  starting transfers between devices  20.7 us (29%)
  local copies, waits for them, and re-layouts  4.04 us (6%)
    all_to_all x1, starting transfers between devices, per_device(): tiles = lax.all_to_all(dev, AXES, 0, 0, tiled=True)  16.3 us
    pallas_call x1, Pallas kernels, per_device(): call(functools.partial(near_kernel, 0), shaped((VECS, LEAF_DEV * LEAF)),...  11.2 us
    pallas_call x1, Pallas kernels, per_device(): call(top_kernel, shaped((VECS, 128)), [SMEM] * 2 + [VMEM] * 2 + [HBM], [p...  7.96 us
    pallas_call x1, Pallas kernels, per_device(): call(functools.partial(near_kernel, 1), shaped((VECS, LEAF_DEV * LEAF)),...  7.12 us
    pallas_call x1, Pallas kernels, per_device(): call(down_kernel, shaped((VECS, LEAF_DEV * LEAF)), [SMEM] * 2 + [VMEM] *...  5.95 us
    pallas_call x1, Pallas kernels, per_device(): call(up_kernel, (shaped((LEAF_DEV, VECS, 128)), shaped((DEVICES, 8, 128))...  4.92 us
    unnamed x20, local copies, waits for them, and re-layouts  4.04 us
    ppermute x1, starting transfers between devices, per_device(): before = lax.ppermute(wide, AXES, up)  3.1 us
  transfers between devices with their start and end apart: 3, of which 0 were waited for; matrix products, arithmetic and copies ran while one was open for 0% of the time, Pallas kernels for 31%

profile of v1, /device:TPU:0, one launch (start us, length us, event | category | flops | bytes accessed | tf_op | source)
XLA Modules:
  0.0 70.0 jit_solution(1007520858271322353)
XLA Ops:
  0.0 4.9 %up.1 = (f32[32,16,128]{2,1,0:T(8,128)S(1)}, f32[128,8,128]{2,1,0:T(8,128)S(1)}, bf16[32,128,128]{2,1,0:T(8,128)(2,1)S(1)}, bf16[32,32,256]{2,1,0:T(8,128)(2,1)S...) custom-call(s32[1]{0:T(128)} %bitcast.1.where, s32[8,32]{1,0:T(8,128)} %bitcast.9, s32[1,32]{1,0:T(1,128)} %bitcast.10, ...), custom_call_target="tpu_custom_call" | custom-call | flops 1000000000 | bytes 1000000 | tf_op jit(solution)/shard_map/up/pallas_call | solution.py:520
  4.9 0.0 copy-start.3
  4.9 0.8 %copy-done.3 = f32[128,8,128]{2,1,0:T(8,128)} copy-done((f32[128,8,128]{2,1,0:T(8,128)}, f32[128,8,128]{2,1,0:T(8,128)S(1)}, u32[]{:S(2)}) %copy-start.3) | copy-done | bytes 524312
  5.7 0.0 copy-start.8
  5.7 0.8 %copy-done.8 = bf16[32,32,256]{2,1,0:T(8,128)(2,1)} copy-done((bf16[32,32,256]{2,1,0:T(8,128)(2,1)}, bf16[32,32,256]{2,1,0:T(8,128)(2,1)S(1)}, u32[]{:S(2)}) %copy-start.8) | copy-done | bytes 524312
  6.5 1.3 %collective-permute-start.1 = (f32[32,8192]{1,0:T(8,128)}, f32[32,8192]{1,0:T(8,128)S(1)}, u32[]{:S(2)}, u32[]{:S(2)}) collective-permute-start(f32[32,8192]{1,0:T(8,128)} %get-tuple-element.25.wide), channel_id=1, source_target_pairs={{1,0},{2,1},{3,2},{4,3},{5,4},{6,5},{7,6},{8,7},{9,8},{10,9},{11,1... | collective-permute-start | bytes 3145736 | tf_op jit(solution)/shard_map/ppermute | solution.py:560
  7.8 3.1 %collective-permute-start = (f32[32,8192]{1,0:T(8,128)}, f32[32,8192]{1,0:T(8,128)S(1)}, u32[]{:S(2)}, u32[]{:S(2)}) collective-permute-start(f32[32,8192]{1,0:T(8,128)} %get-tuple-element.25.wide), channel_id=1, source_target_pairs={{0,1},{1,2},{2,3},{3,4},{4,5},{5,6},{6,7},{7,8},{8,9},{9,10},{10,1... | collective-permute-start | bytes 3145736 | tf_op jit(solution)/shard_map/ppermute | solution.py:559
  10.9 16.3 %all-to-all-start = ((f32[128,8,128]{2,1,0:T(8,128)}), f32[128,8,128]{2,1,0:T(8,128)}, u32[]{:S(2)}, u32[]{:S(2)}) async-start(f32[128,8,128]{2,1,0:T(8,128)} %copy-done.3), calls=%async_computation | async-start | bytes 1048576 | tf_op jit(solution)/shard_map/all_to_all | solution.py:558
  27.2 0.0 copy-start.9
  27.2 2.4 %own.1 = (bf16[8,256,128]{2,1,0:T(8,128)(2,1)S(1)}, bf16[32,224,256]{2,1,0:T(8,128)(2,1)S(1)}) custom-call(f32[32,8192]{1,0:T(8,128)} %get-tuple-element.25.wide), custom_call_target="tpu_custom_call" | custom-call | flops 2000000000 | bytes 2000000 | tf_op jit(solution)/shard_map/own/pallas_call | solution.py:561
  29.6 0.0 copy-done.9
  29.6 11.2 %near0.1.rest_0_ = f32[16,8192]{1,0:T(8,128)S(1)} custom-call(s32[1,384]{1,0:T(1,128)S(1)} %get-tuple-element.23.pairs, bf16[32,32,256]{2,1,0:T(8,128)(2,1)S(1)} %copy-done.9, bf16[8,256,128]{2,1,0:T(8,128)(2,1)S(1)} %get-tuple-element.26.partner.partner_own, bf16[32,224,256]{2,1,0:T(8,128)(2,1)S(1)} %get-tuple-element.27.own), custom_call_target="tpu_custom_call" | custom-call | flops 8000000000 | bytes 8000000 | tf_op jit(solution)/shard_map/near0/pallas_call | solution.py:572
  40.9 0.0 collective-permute-done.1.after
  40.9 0.0 collective-permute-done.before
  40.9 1.0 %other.1 = (bf16[97,32,256]{2,1,0:T(8,128)(2,1)S(1)}, bf16[25,256,128]{2,1,0:T(8,128)(2,1)S(1)}) custom-call(bf16[32,32,256]{2,1,0:T(8,128)(2,1)S(1)} %copy-done.9, bf16[8,256,128]{2,1,0:T(8,128)(2,1)S(1)} %get-tuple-element.26.partner.partner_own, f32[32,8192]{1,0:T(8,128)S(1)} %collective-permute-done.before, f32[32,8192]{1,0:T(8,128)S(1)} %collective-permute-done.1.after), custom_call_target="tpu_custom_call" | custom-call | flops 2000000000 | bytes 2000000 | tf_op jit(solution)/shard_map/other/pallas_call | solution.py:581
  41.9 7.1 %near1.1.near = f32[16,8192]{1,0:T(8,128)S(1)} custom-call(s32[1,384]{1,0:T(1,128)S(1)} %get-tuple-element.23.pairs, bf16[97,32,256]{2,1,0:T(8,128)(2,1)S(1)} %get-tuple-element.31.xs, bf16[25,256,128]{2,1,0:T(8,128)(2,1)S(1)} %get-tuple-element.32.partner, bf16[32,224,256]{2,1,0:T(8,128)(2,1)S(1)} %get-tuple-element.27.own, f32[16,8192]{1,0:T(8,128)S(1)} %near0.1.rest_0_), custom_call_target="tpu_custom_call" | custom-call | flops 8000000000 | bytes 8000000 | tf_op jit(solution)/shard_map/near1/pallas_call | solution.py:592
  49.0 0.8 %copy-done.1 = f32[16,8192]{1,0:T(8,128)} copy-done((f32[16,8192]{1,0:T(8,128)}, f32[16,8192]{1,0:T(8,128)S(1)}, u32[]{:S(2)}) %copy-start.1) | copy-done | bytes 524312
  49.8 0.0 all-to-all-done.tiles_in
  49.8 1.6 %copy-done.6 = bf16[256,4096]{1,0:T(8,128)(2,1)S(1)} copy-done((bf16[256,4096]{1,0:T(8,128)(2,1)S(1)}, bf16[256,4096]{1,0:T(8,128)(2,1)}, u32[]{:S(2)}) %copy-start.6) | copy-done | bytes 2097176
  51.4 2.4 %pack.1.ee = bf16[128,128,128]{2,1,0:T(8,128)(2,1)S(1)} custom-call(bf16[256,4096]{1,0:T(8,128)(2,1)S(1)} %copy-done.6), custom_call_target="tpu_custom_call" | custom-call | flops 4000000000 | bytes 4000000 | tf_op jit(solution)/shard_map/pack/pallas_call | solution.py:602
  53.9 0.0 copy-done.5
  53.9 0.0 copy-start.7
  53.9 2.1 %blocks.1 = bf16[64,384,128]{2,1,0:T(8,128)(2,1)S(1)} custom-call(bf16[6,64,4096]{2,1,0:T(8,128)(2,1)S(1)} %bitcast.7), custom_call_target="tpu_custom_call" | custom-call | flops 3000000000 | bytes 3000000 | tf_op jit(solution)/shard_map/blocks/pallas_call | solution.py:625
  56.0 0.0 copy-done.7
  56.0 0.0 copy-start
  56.1 0.0 copy-start.2
  56.1 0.0 copy-start.4
  56.1 8.0 %top.1.path = f32[16,128]{1,0:T(8,128)S(1)} custom-call(s32[2,256]{1,0:T(2,128)S(1)} %bitcast.8, s32[1]{0:T(128)} %bitcast.1.where, f32[128,8,128]{2,1,0:T(8,128)} %all-to-all-done.tiles_in, bf16[128,128,128]{2,1,0:T(8,128)(2,1)S(1)} %pack.1.ee, bf16[256,2,4096]{2,1,0:T(2,128)(2,1)} %coupling.1), custom_call_target="tpu_custom_call" | custom-call | flops 6000000000 | bytes 6000000 | tf_op jit(solution)/shard_map/top/pallas_call | solution.py:606
  64.0 0.0 copy-done
  64.1 0.0 copy-done.2
  64.1 0.0 copy-done.4
  64.1 6.0 %down.1 = f32[16,8192]{1,0:T(8,128)} custom-call(s32[6,64]{1,0:T(8,128)S(1)} %bitcast.6, s32[1]{0:T(128)} %bitcast.1.where, f32[32,16,128]{2,1,0:T(8,128)S(1)} %get-tuple-element.22.sk_own, f32[32,8192]{1,0:T(8,128)S(1)} %collective-permute-done.before, f32[32,8192]{1,0:T(8,128)S(1)} %collective-permute-done.1.after, bf16[64,384,128]{2,1,0:T(8,128)(2,1)S(1)} %blocks.1, ...), custom_call_target="tpu_custom_call" | custom-call | flops 1000000000 | bytes 1000000 | tf_op jit(solution)/shard_map/down/pallas_call | solution.py:633
  (3 shorter events, 0.0 us)
Async XLA Ops:
  4.9 0.8 %copy-start.3 = (f32[128,8,128]{2,1,0:T(8,128)}, f32[128,8,128]{2,1,0:T(8,128)S(1)}, u32[]{:S(2)}) copy-start(f32[128,8,128]{2,1,0:T(8,128)S(1)} %get-tuple-element.30) | copy-start | bytes 1572868
  5.7 0.8 %copy-start.8 = (bf16[32,32,256]{2,1,0:T(8,128)(2,1)}, bf16[32,32,256]{2,1,0:T(8,128)(2,1)S(1)}, u32[]{:S(2)}) copy-start(bf16[32,32,256]{2,1,0:T(8,128)(2,1)S(1)} %get-tuple-element.24.xs.xs_own) | copy-start | bytes 1572868
  6.5 34.3 %collective-permute-start.1 = (f32[32,8192]{1,0:T(8,128)}, f32[32,8192]{1,0:T(8,128)S(1)}, u32[]{:S(2)}, u32[]{:S(2)}) collective-permute-start(f32[32,8192]{1,0:T(8,128)} %get-tuple-element.25.wide), channel_id=1, source_target_pairs={{1,0},{2,1},{3,2},{4,3},{5,4},{6,5},{7,6},{8,7},{9,8},{10,9},{11,1... | collective-permute-start | bytes 3145736 | tf_op jit(solution)/shard_map/ppermute | solution.py:560
  7.8 33.1 %collective-permute-start = (f32[32,8192]{1,0:T(8,128)}, f32[32,8192]{1,0:T(8,128)S(1)}, u32[]{:S(2)}, u32[]{:S(2)}) collective-permute-start(f32[32,8192]{1,0:T(8,128)} %get-tuple-element.25.wide), channel_id=1, source_target_pairs={{0,1},{1,2},{2,3},{3,4},{4,5},{5,6},{6,7},{7,8},{8,9},{9,10},{10,1... | collective-permute-start | bytes 3145736 | tf_op jit(solution)/shard_map/ppermute | solution.py:559
  10.9 38.9 %all-to-all-start = ((f32[128,8,128]{2,1,0:T(8,128)}), f32[128,8,128]{2,1,0:T(8,128)}, u32[]{:S(2)}, u32[]{:S(2)}) async-start(f32[128,8,128]{2,1,0:T(8,128)} %copy-done.3), calls=%async_computation | async-start | bytes 1048576 | tf_op jit(solution)/shard_map/all_to_all | solution.py:558
  27.2 2.4 %copy-start.9 = (bf16[32,32,256]{2,1,0:T(8,128)(2,1)S(1)}, bf16[32,32,256]{2,1,0:T(8,128)(2,1)}, u32[]{:S(2)}) copy-start(bf16[32,32,256]{2,1,0:T(8,128)(2,1)} %copy-done.8) | copy-start | bytes 1572868
  49.0 0.8 %copy-start.1 = (f32[16,8192]{1,0:T(8,128)}, f32[16,8192]{1,0:T(8,128)S(1)}, u32[]{:S(2)}) copy-start(f32[16,8192]{1,0:T(8,128)S(1)} %near1.1.near) | copy-start | bytes 1572868
  49.8 1.6 %copy-start.6 = (bf16[256,4096]{1,0:T(8,128)(2,1)S(1)}, bf16[256,4096]{1,0:T(8,128)(2,1)}, u32[]{:S(2)}) copy-start(bf16[256,4096]{1,0:T(8,128)(2,1)} %transfer) | copy-start | bytes 6291460
  51.4 2.4 %copy-start.5 = (bf16[64,6,4096]{2,0,1:T(8,128)(2,1)S(1)}, bf16[64,6,4096]{2,0,1:T(8,128)(2,1)}, u32[]{:S(2)}) copy-start(bf16[64,6,4096]{2,0,1:T(8,128)(2,1)} %param.15) | copy-start | bytes 9437188
  53.9 2.2 %copy-start.7 = (s32[256,2]{0,1:T(2,128)S(1)}, s32[256,2]{0,1:T(2,128)}, u32[]{:S(2)}) copy-start(s32[256,2]{0,1:T(2,128)} %param.21) | copy-start | bytes 6148
  56.0 8.0 %copy-start = (bf16[32,64,256]{2,1,0:T(8,128)(2,1)S(1)}, bf16[32,64,256]{2,1,0:T(8,128)(2,1)}, u32[]{:S(2)}) copy-start(bf16[32,64,256]{2,1,0:T(8,128)(2,1)} %basis.1) | copy-start | bytes 3145732
  56.1 8.0 %copy-start.2 = (f32[16,8192]{1,0:T(8,128)S(1)}, f32[16,8192]{1,0:T(8,128)}, u32[]{:S(2)}) copy-start(f32[16,8192]{1,0:T(8,128)} %copy-done.1) | copy-start | bytes 1572868
  56.1 8.0 %copy-start.4 = (s32[64,6]{0,1:T(8,128)S(1)}, s32[64,6]{0,1:T(8,128)}, u32[]{:S(2)}) copy-start(s32[64,6]{0,1:T(8,128)} %param.18) | copy-start | bytes 4612
